TPU v7x, 128 devices: a whole 4x4x4 slice. The times are simulated.
128 devices in a mesh: tiles: 64 (over y, z_hi, x, core), vec: 2 (over z_lo).
Axes of the slice: x: 4, y: 4, z: 4 (z_hi: 2, z_lo: 2; z = z_hi * 2 + z_lo), core: 2. Of those that a mesh axis runs over, the one named last changes fastest.
Arguments:
- omega: float32 [128, 4, 512, 128], P('vec', None, 'tiles'), may hold values from -24 to 24
- conductance: float32 [3, 4, 512, 128], P(None, None, 'tiles'), may hold values from 0.02 to 0.16
- wet: int32 [512, 128], P('tiles'), may hold values 0 or 1
- volume: float32 [512, 128], P('tiles'), may hold values from 0.3 to 27, as said below
- face_runs: int32 [64, 4], P('tiles'), may hold values from 0 to 128, as said below
Outputs:
- diffused: float32 [128, 4, 512, 128], P('vec', None, 'tiles')
- r_factor: float32 [128, 128], replicated
Inputs may be any that keep to these rules, and one draw needn't show every extreme that they name: `face_runs`: tiles in tile row 0 have a closed lower row face and tiles in tile column 0 a closed lower column face (length 0); every other run lies within its face, covers at least half of it, and some tiles have fully open faces. Positive cell volume weights.
All inputs are finite; a program needn't handle non-finite values. No bound on the sum of `wet` on one device may be relied on, other than what follows from the above.
Results may differ from a plain program's by a relative error of at most 0.00005.
Values sent between devices are 32-bit elements; how exact they have to be, the bound alone decides.
A program may use at most 64 MiB of HBM per device.

v0:
```python
import jax
import jax.numpy as jnp
from jax import lax
from jax.sharding import PartitionSpec as P

TGY = 8
ITERS = 4


def shifted(value, axis, steps):
    count = lax.axis_size(axis)
    first, last = (max(0, -steps), min(count, count - steps))
    return lax.ppermute(value, axis, [(source, source + steps) for source in range(first, last)])


def diffuse(field, statics):
    cond_x = statics[0]
    cond_y = statics[1]
    cond_z = statics[2]
    wet_cells = statics[3]
    flux_x = cond_x[:, 1:, :] * (field[:, :, 1:, :] - field[:, :, :-1, :])
    flux_y = cond_y[:, :, 1:] * (field[:, :, :, 1:] - field[:, :, :, :-1])
    flux_z = cond_z[1:] * (field[:, 1:] - field[:, :-1])
    zero_level = jnp.zeros_like(field[:, :1])
    flux_z = jnp.concatenate([zero_level, flux_z, zero_level], axis=1)
    change = flux_x[:, :, 1:, 1:-1] - flux_x[:, :, :-1, 1:-1]
    change = change + flux_y[:, :, 1:-1, 1:] - flux_y[:, :, 1:-1, :-1]
    change = change + (flux_z[:, 1:] - flux_z[:, :-1])[:, :, 1:-1, 1:-1]
    return wet_cells[:, 1:-1, 1:-1] * (field[:, :, 1:-1, 1:-1] + change)


def moving(values, offset):
    return shifted(values, "tiles", offset)


def fixed_rim(values, offset):
    return shifted(values, "tiles", offset)


def extend(values, margin, neighbour):
    lower_rim = neighbour(values[:, :, -margin:, :], TGY)
    upper_rim = neighbour(values[:, :, :margin, :], -TGY)
    stacked = jnp.concatenate([lower_rim, values, upper_rim], axis=2)
    left_rim = neighbour(stacked[:, :, :, -margin:], 1)
    right_rim = neighbour(stacked[:, :, :, :margin], -1)
    return jnp.concatenate([left_rim, stacked, right_rim], axis=3)


def shards(omega, conductance, wet, volume, face_runs):
    levels = omega.shape[1]
    tile_rows = omega.shape[2]
    tile_cols = omega.shape[3]
    row_ids = lax.broadcasted_iota(jnp.int32, (tile_rows, tile_cols), 0)
    col_ids = lax.broadcasted_iota(jnp.int32, (tile_rows, tile_cols), 1)
    runs = face_runs[0]
    open_x = (col_ids >= runs[0]) & (col_ids < runs[0] + runs[1])
    factor_x = jnp.where(row_ids == 0, open_x.astype(jnp.float32), jnp.float32(1.0))
    open_y = (row_ids >= runs[2]) & (row_ids < runs[2] + runs[3])
    factor_y = jnp.where(col_ids == 0, open_y.astype(jnp.float32), jnp.float32(1.0))
    level_ids = lax.broadcasted_iota(jnp.int32, (levels, 1, 1), 0)
    cond_z = conductance[2] * (level_ids > 0).astype(jnp.float32)
    wet_float = wet.astype(jnp.float32)
    statics = jnp.stack(
        [
            conductance[0] * factor_x[None],
            conductance[1] * factor_y[None],
            cond_z,
            jnp.broadcast_to(wet_float[None], (levels, tile_rows, tile_cols)),
        ]
    )
    margin = 1
    statics_wide = extend(statics, margin, fixed_rim)
    field = wet_float[None, None] * omega
    for block_index in range(ITERS // margin):
        grown = extend(field, margin, moving)
        current = statics_wide
        grown = diffuse(grown, current)
        current = current[:, :, 1:-1, 1:-1]
        field = grown
    regrouped = lax.all_to_all(field, "vec", split_axis=1, concat_axis=0, tiled=True)
    all_vectors = regrouped.shape[0]
    total_cells = levels * lax.axis_size("tiles") * tile_rows * tile_cols
    flat_values = regrouped.reshape(all_vectors, -1)
    weighted = (regrouped * volume[None, None]).reshape(all_vectors, -1)
    gram_local = (
        lax.dot_general(
            weighted,
            flat_values,
            (((1,), (1,)), ((), ())),
            precision=lax.Precision.HIGHEST,
            preferred_element_type=jnp.float32,
        )
        / total_cells
    )
    gram = lax.psum(gram_local, ("tiles", "vec"))
    r_factor = jnp.linalg.cholesky(gram).T
    return (field, r_factor)


def solution(mesh):
    in_specs = (
        P("vec", None, "tiles", None),
        P(None, None, "tiles", None),
        P("tiles", None),
        P("tiles", None),
        P("tiles", None),
    )
    out_specs = (P("vec", None, "tiles", None), P())
    return jax.shard_map(shards, mesh=mesh, in_specs=in_specs, out_specs=out_specs, check_vma=False)
```

profile of v0, /device:TPU:1, one launch (start us, length us, event | category | flops | bytes accessed | tf_op | source)
XLA Modules:
  0.0 363.9 jit_solution(15413979670254158427)
XLA Ops:
  7.2 1.5 fusion.34
  14.1 6.3 %collective-permute-start = (f32[4,4,1,128]{3,2,1,0:T(1,128)S(1)}, f32[4,4,1,128]{3,2,1,0:T(1,128)S(1)}, u32[]{:S(2)}, u32[]{:S(2)}) collective-permute-start(f32[4,4,1,128]{3,2,1,0:T(1,128)S(1)} %get-tuple-element.29), channel_id=1, source_target_pairs={{0,16},{2,18},{4,20},{6,22},{8,24},{10,26},{12,28},{14,30},{16,32}... | collective-permute-start | bytes 24584 | tf_op jit(solution)/shard_map/ppermute | solution.py:13
  21.7 1.8 copy_multiply_fusion
  23.6 2.7 collective-permute-done.1
  26.4 5.1 %collective-permute-start.2 = (f32[4,4,10,1]{3,2,1,0:T(8,128)S(1)}, f32[4,4,10,1]{3,2,1,0:T(8,128)S(1)}, u32[]{:S(2)}, u32[]{:S(2)}) collective-permute-start(f32[4,4,10,1]{3,2,1,0:T(8,128)S(1)} %get-tuple-element.27), channel_id=1, source_target_pairs={{0,2},{2,4},{4,6},{6,8},{8,10},{10,12},{12,14},{14,16},{16,18},{18... | collective-permute-start | bytes 1928 | tf_op jit(solution)/shard_map/ppermute | solution.py:13
  31.6 1.9 collective-permute-start.3
  33.5 3.2 collective-permute-start.4
  38.6 5.3 %collective-permute-done.5 = f32[64,4,1,128]{3,0,2,1:T(8,128)S(1)} collective-permute-done((f32[64,4,1,128]{3,0,2,1:T(8,128)S(1)}, f32[64,4,1,128]{3,0,2,1:T(8,128)S(1)}, u32[]{:S(2)}, u32[]{:S(2)}) %collective-permute-start.5) | collective-permute-done | bytes 131104 | tf_op jit(solution)/shard_map/ppermute | solution.py:13
  44.0 1.5 fusion.28
  45.6 2.0 copy.15
  48.3 8.0 %collective-permute-start.7 = (f32[64,4,10,1]{0,2,3,1:T(8,128)S(1)}, f32[64,4,10,1]{0,2,3,1:T(8,128)S(1)}, u32[]{:S(2)}, u32[]{:S(2)}) collective-permute-start(f32[64,4,10,1]{0,2,3,1:T(8,128)S(1)} %copy.16), channel_id=1, source_target_pairs={{2,0},{4,2},{6,4},{8,6},{10,8},{12,10},{14,12},{16,14},{18,16},{20... | collective-permute-start | bytes 30728 | tf_op jit(solution)/shard_map/ppermute | solution.py:13
  56.2 1.9 collective-permute-start.6
  59.8 1.6 copy.18
  61.4 2.4 pad_maximum_fusion
  66.7 1.3 fusion.23
  68.0 6.0 %collective-permute-start.8 = (f32[64,4,1,128]{3,0,2,1:T(8,128)S(1)}, f32[64,4,1,128]{3,0,2,1:T(8,128)S(1)}, u32[]{:S(2)}, u32[]{:S(2)}) collective-permute-start(f32[64,4,1,128]{3,0,2,1:T(8,128)S(1)} %get-tuple-element.20), channel_id=1, source_target_pairs={{0,16},{2,18},{4,20},{6,22},{8,24},{10,26},{12,28},{14,30},{16,32}... | collective-permute-start | bytes 393224 | tf_op jit(solution)/shard_map/ppermute | solution.py:13
  76.0 5.3 %collective-permute-done.9 = f32[64,4,1,128]{3,0,2,1:T(8,128)S(1)} collective-permute-done((f32[64,4,1,128]{3,0,2,1:T(8,128)S(1)}, f32[64,4,1,128]{3,0,2,1:T(8,128)S(1)}, u32[]{:S(2)}, u32[]{:S(2)}) %collective-permute-start.9) | collective-permute-done | bytes 131104 | tf_op jit(solution)/shard_map/ppermute | solution.py:13
  81.4 1.5 fusion.27
  82.9 2.0 copy.21
  84.9 5.5 %collective-permute-start.10 = (f32[64,4,10,1]{0,2,3,1:T(8,128)S(1)}, f32[64,4,10,1]{0,2,3,1:T(8,128)S(1)}, u32[]{:S(2)}, u32[]{:S(2)}) collective-permute-start(f32[64,4,10,1]{0,2,3,1:T(8,128)S(1)} %copy.21), channel_id=1, source_target_pairs={{0,2},{2,4},{4,6},{6,8},{8,10},{10,12},{12,14},{14,16},{16,18},{18... | collective-permute-start | bytes 30728 | tf_op jit(solution)/shard_map/ppermute | solution.py:13
  91.1 5.1 %collective-permute-start.11 = (f32[64,4,10,1]{0,2,3,1:T(8,128)S(1)}, f32[64,4,10,1]{0,2,3,1:T(8,128)S(1)}, u32[]{:S(2)}, u32[]{:S(2)}) collective-permute-start(f32[64,4,10,1]{0,2,3,1:T(8,128)S(1)} %copy.22), channel_id=1, source_target_pairs={{2,0},{4,2},{6,4},{8,6},{10,8},{12,10},{14,12},{16,14},{18,16},{20... | collective-permute-start | bytes 30728 | tf_op jit(solution)/shard_map/ppermute | solution.py:13
  96.9 1.6 copy.24
  98.4 2.4 pad_maximum_fusion.1
  103.3 1.3 fusion.20
  104.7 4.5 %collective-permute-start.12 = (f32[64,4,1,128]{3,0,2,1:T(8,128)S(1)}, f32[64,4,1,128]{3,0,2,1:T(8,128)S(1)}, u32[]{:S(2)}, u32[]{:S(2)}) collective-permute-start(f32[64,4,1,128]{3,0,2,1:T(8,128)S(1)} %get-tuple-element.18), channel_id=1, source_target_pairs={{0,16},{2,18},{4,20},{6,22},{8,24},{10,26},{12,28},{14,30},{16,32}... | collective-permute-start | bytes 393224 | tf_op jit(solution)/shard_map/ppermute | solution.py:13
  111.1 5.3 %collective-permute-done.13 = f32[64,4,1,128]{3,0,2,1:T(8,128)S(1)} collective-permute-done((f32[64,4,1,128]{3,0,2,1:T(8,128)S(1)}, f32[64,4,1,128]{3,0,2,1:T(8,128)S(1)}, u32[]{:S(2)}, u32[]{:S(2)}) %collective-permute-start.13) | collective-permute-done | bytes 131104 | tf_op jit(solution)/shard_map/ppermute | solution.py:13
  116.5 1.5 fusion.26
  118.0 2.0 copy.27
  120.0 1.9 collective-permute-start.14
  122.6 8.8 %collective-permute-start.15 = (f32[64,4,10,1]{0,2,3,1:T(8,128)S(1)}, f32[64,4,10,1]{0,2,3,1:T(8,128)S(1)}, u32[]{:S(2)}, u32[]{:S(2)}) collective-permute-start(f32[64,4,10,1]{0,2,3,1:T(8,128)S(1)} %copy.28), channel_id=1, source_target_pairs={{2,0},{4,2},{6,4},{8,6},{10,8},{12,10},{14,12},{16,14},{18,16},{20... | collective-permute-start | bytes 30728 | tf_op jit(solution)/shard_map/ppermute | solution.py:13
  132.3 1.6 copy.30
  133.8 2.4 pad_maximum_fusion.2
  138.8 1.3 fusion.17
  140.1 6.4 %collective-permute-start.16 = (f32[64,4,1,128]{3,0,2,1:T(8,128)S(1)}, f32[64,4,1,128]{3,0,2,1:T(8,128)S(1)}, u32[]{:S(2)}, u32[]{:S(2)}) collective-permute-start(f32[64,4,1,128]{3,0,2,1:T(8,128)S(1)} %get-tuple-element.16), channel_id=1, source_target_pairs={{0,16},{2,18},{4,20},{6,22},{8,24},{10,26},{12,28},{14,30},{16,32}... | collective-permute-start | bytes 393224 | tf_op jit(solution)/shard_map/ppermute | solution.py:13
  148.4 5.3 %collective-permute-done.17 = f32[64,4,1,128]{3,0,2,1:T(8,128)S(1)} collective-permute-done((f32[64,4,1,128]{3,0,2,1:T(8,128)S(1)}, f32[64,4,1,128]{3,0,2,1:T(8,128)S(1)}, u32[]{:S(2)}, u32[]{:S(2)}) %collective-permute-start.17) | collective-permute-done | bytes 131104 | tf_op jit(solution)/shard_map/ppermute | solution.py:13
  153.8 1.5 fusion.25
  155.3 2.0 copy.33
  157.3 1.9 collective-permute-start.18
  159.9 9.0 %collective-permute-start.19 = (f32[64,4,10,1]{0,2,3,1:T(8,128)S(1)}, f32[64,4,10,1]{0,2,3,1:T(8,128)S(1)}, u32[]{:S(2)}, u32[]{:S(2)}) collective-permute-start(f32[64,4,10,1]{0,2,3,1:T(8,128)S(1)} %copy.34), channel_id=1, source_target_pairs={{2,0},{4,2},{6,4},{8,6},{10,8},{12,10},{14,12},{16,14},{18,16},{20... | collective-permute-start | bytes 30728 | tf_op jit(solution)/shard_map/ppermute | solution.py:13
  169.6 1.6 copy.36
  171.1 2.4 pad_maximum_fusion.3
  176.0 1.3 fusion.14
  178.0 15.8 %all_to_all.15 = f32[64,4,8,128]{3,2,0,1:T(8,128)S(1)} all-to-all(f32[64,4,8,128]{3,2,0,1:T(8,128)S(1)} %copy.39), channel_id=1, replica_groups=mesh['tiles'=64,'vec'=2] {'vec'}, dimensions={1} | all-to-all | bytes 2097152 | tf_op jit(solution)/shard_map/all_to_all | solution.py:80
  194.9 1.4 reshape.96
  197.5 2.9 convolution_multiply_fusion
  200.3 1.6 copy.43
  201.9 139.6 %all-reduce.10.cloned.1.call-done = f32[128,128]{0,1:T(8,128)} async-done(((f32[128,128]{0,1:T(8,128)}), f32[128,128]{0,1:T(8,128)}) %all-reduce.10.cloned.1.call-update) | async-done | bytes 65552 | tf_op jit(solution)/shard_map/psum | solution.py:95
  343.3 11.7 %cholesky.18 = f32[128,128]{1,0:T(8,128)S(1)} custom-call(f32[128,128]{1,0:T(8,128)S(1)} %fusion.24), custom_call_target="Cholesky" | custom-call | tf_op jit(solution)/shard_map/jit(cholesky)/cholesky | solution.py:96
  (96 shorter events, 35.8 us)
Async XLA Ops:
  7.2 334.3 %all-reduce.10.cloned.1.call-start = ((), (), s32[]{:S(2)}) async-start(), calls=%async_computation.1 | async-start | bytes 131072 | tf_op jit(solution)/shard_map/psum | solution.py:95
  14.1 9.5 %collective-permute-start = (f32[4,4,1,128]{3,2,1,0:T(1,128)S(1)}, f32[4,4,1,128]{3,2,1,0:T(1,128)S(1)}, u32[]{:S(2)}, u32[]{:S(2)}) collective-permute-start(f32[4,4,1,128]{3,2,1,0:T(1,128)S(1)} %get-tuple-element.29), channel_id=1, source_target_pairs={{0,16},{2,18},{4,20},{6,22},{8,24},{10,26},{12,28},{14,30},{16,32}... | collective-permute-start | bytes 24584 | tf_op jit(solution)/shard_map/ppermute | solution.py:13
  20.4 5.9 %collective-permute-start.1 = (f32[4,4,1,128]{3,2,1,0:T(1,128)S(1)}, f32[4,4,1,128]{3,2,1,0:T(1,128)S(1)}, u32[]{:S(2)}, u32[]{:S(2)}) collective-permute-start(f32[4,4,1,128]{3,2,1,0:T(1,128)S(1)} %get-tuple-element.30), channel_id=1, source_target_pairs={{16,0},{18,2},{20,4},{22,6},{24,8},{26,10},{28,12},{30,14},{32,16}... | collective-permute-start | bytes 24584 | tf_op jit(solution)/shard_map/ppermute | solution.py:13
  26.4 11.6 %collective-permute-start.2 = (f32[4,4,10,1]{3,2,1,0:T(8,128)S(1)}, f32[4,4,10,1]{3,2,1,0:T(8,128)S(1)}, u32[]{:S(2)}, u32[]{:S(2)}) collective-permute-start(f32[4,4,10,1]{3,2,1,0:T(8,128)S(1)} %get-tuple-element.27), channel_id=1, source_target_pairs={{0,2},{2,4},{4,6},{6,8},{8,10},{10,12},{12,14},{14,16},{16,18},{18... | collective-permute-start | bytes 1928 | tf_op jit(solution)/shard_map/ppermute | solution.py:13
  31.6 6.5 %collective-permute-start.3 = (f32[4,4,10,1]{3,2,1,0:T(8,128)S(1)}, f32[4,4,10,1]{3,2,1,0:T(8,128)S(1)}, u32[]{:S(2)}, u32[]{:S(2)}) collective-permute-start(f32[4,4,10,1]{3,2,1,0:T(8,128)S(1)} %get-tuple-element.28), channel_id=1, source_target_pairs={{2,0},{4,2},{6,4},{8,6},{10,8},{12,10},{14,12},{16,14},{18,16},{20... | collective-permute-start | bytes 1928 | tf_op jit(solution)/shard_map/ppermute | solution.py:13
  33.5 5.1 %collective-permute-start.4 = (f32[64,4,1,128]{3,0,2,1:T(8,128)S(1)}, f32[64,4,1,128]{3,0,2,1:T(8,128)S(1)}, u32[]{:S(2)}, u32[]{:S(2)}) collective-permute-start(f32[64,4,1,128]{3,0,2,1:T(8,128)S(1)} %get-tuple-element.22), channel_id=1, source_target_pairs={{0,16},{2,18},{4,20},{6,22},{8,24},{10,26},{12,28},{14,30},{16,32}... | collective-permute-start | bytes 393224 | tf_op jit(solution)/shard_map/ppermute | solution.py:13
  36.7 7.2 %collective-permute-start.5 = (f32[64,4,1,128]{3,0,2,1:T(8,128)S(1)}, f32[64,4,1,128]{3,0,2,1:T(8,128)S(1)}, u32[]{:S(2)}, u32[]{:S(2)}) collective-permute-start(f32[64,4,1,128]{3,0,2,1:T(8,128)S(1)} %get-tuple-element.23), channel_id=1, source_target_pairs={{16,0},{18,2},{20,4},{22,6},{24,8},{26,10},{28,12},{30,14},{32,16}... | collective-permute-start | bytes 393224 | tf_op jit(solution)/shard_map/ppermute | solution.py:13
  48.3 11.5 %collective-permute-start.7 = (f32[64,4,10,1]{0,2,3,1:T(8,128)S(1)}, f32[64,4,10,1]{0,2,3,1:T(8,128)S(1)}, u32[]{:S(2)}, u32[]{:S(2)}) collective-permute-start(f32[64,4,10,1]{0,2,3,1:T(8,128)S(1)} %copy.16), channel_id=1, source_target_pairs={{2,0},{4,2},{6,4},{8,6},{10,8},{12,10},{14,12},{16,14},{18,16},{20... | collective-permute-start | bytes 30728 | tf_op jit(solution)/shard_map/ppermute | solution.py:13
  56.2 3.1 collective-permute-start.6
  58.2 42.7 %copy-start.5 = (f32[3,10,130]{2,1,0:T(8,128)}, f32[3,10,130]{2,1,0:T(8,128)S(1)}, u32[]{:S(2)}) copy-start(f32[3,10,130]{2,1,0:T(8,128)S(1)} %slice_bitcast_fusion.3) | copy-start | bytes 46804
  64.1 1.3 copy-start.1
  65.5 1.2 copy-start.4
  68.0 8.0 %collective-permute-start.8 = (f32[64,4,1,128]{3,0,2,1:T(8,128)S(1)}, f32[64,4,1,128]{3,0,2,1:T(8,128)S(1)}, u32[]{:S(2)}, u32[]{:S(2)}) collective-permute-start(f32[64,4,1,128]{3,0,2,1:T(8,128)S(1)} %get-tuple-element.20), channel_id=1, source_target_pairs={{0,16},{2,18},{4,20},{6,22},{8,24},{10,26},{12,28},{14,30},{16,32}... | collective-permute-start | bytes 393224 | tf_op jit(solution)/shard_map/ppermute | solution.py:13
  74.1 7.2 %collective-permute-start.9 = (f32[64,4,1,128]{3,0,2,1:T(8,128)S(1)}, f32[64,4,1,128]{3,0,2,1:T(8,128)S(1)}, u32[]{:S(2)}, u32[]{:S(2)}) collective-permute-start(f32[64,4,1,128]{3,0,2,1:T(8,128)S(1)} %get-tuple-element.21), channel_id=1, source_target_pairs={{16,0},{18,2},{20,4},{22,6},{24,8},{26,10},{28,12},{30,14},{32,16}... | collective-permute-start | bytes 393224 | tf_op jit(solution)/shard_map/ppermute | solution.py:13
  84.9 11.3 %collective-permute-start.10 = (f32[64,4,10,1]{0,2,3,1:T(8,128)S(1)}, f32[64,4,10,1]{0,2,3,1:T(8,128)S(1)}, u32[]{:S(2)}, u32[]{:S(2)}) collective-permute-start(f32[64,4,10,1]{0,2,3,1:T(8,128)S(1)} %copy.21), channel_id=1, source_target_pairs={{0,2},{2,4},{4,6},{6,8},{8,10},{10,12},{12,14},{14,16},{16,18},{18... | collective-permute-start | bytes 30728 | tf_op jit(solution)/shard_map/ppermute | solution.py:13
  91.1 5.8 %collective-permute-start.11 = (f32[64,4,10,1]{0,2,3,1:T(8,128)S(1)}, f32[64,4,10,1]{0,2,3,1:T(8,128)S(1)}, u32[]{:S(2)}, u32[]{:S(2)}) collective-permute-start(f32[64,4,10,1]{0,2,3,1:T(8,128)S(1)} %copy.22), channel_id=1, source_target_pairs={{2,0},{4,2},{6,4},{8,6},{10,8},{12,10},{14,12},{16,14},{18,16},{20... | collective-permute-start | bytes 30728 | tf_op jit(solution)/shard_map/ppermute | solution.py:13
  101.2 1.3 copy-start.2
  104.7 6.4 %collective-permute-start.12 = (f32[64,4,1,128]{3,0,2,1:T(8,128)S(1)}, f32[64,4,1,128]{3,0,2,1:T(8,128)S(1)}, u32[]{:S(2)}, u32[]{:S(2)}) collective-permute-start(f32[64,4,1,128]{3,0,2,1:T(8,128)S(1)} %get-tuple-element.18), channel_id=1, source_target_pairs={{0,16},{2,18},{4,20},{6,22},{8,24},{10,26},{12,28},{14,30},{16,32}... | collective-permute-start | bytes 393224 | tf_op jit(solution)/shard_map/ppermute | solution.py:13
  109.2 7.2 %collective-permute-start.13 = (f32[64,4,1,128]{3,0,2,1:T(8,128)S(1)}, f32[64,4,1,128]{3,0,2,1:T(8,128)S(1)}, u32[]{:S(2)}, u32[]{:S(2)}) collective-permute-start(f32[64,4,1,128]{3,0,2,1:T(8,128)S(1)} %get-tuple-element.19), channel_id=1, source_target_pairs={{16,0},{18,2},{20,4},{22,6},{24,8},{26,10},{28,12},{30,14},{32,16}... | collective-permute-start | bytes 393224 | tf_op jit(solution)/shard_map/ppermute | solution.py:13
  120.0 11.4 %collective-permute-start.14 = (f32[64,4,10,1]{0,2,3,1:T(8,128)S(1)}, f32[64,4,10,1]{0,2,3,1:T(8,128)S(1)}, u32[]{:S(2)}, u32[]{:S(2)}) collective-permute-start(f32[64,4,10,1]{0,2,3,1:T(8,128)S(1)} %copy.27), channel_id=1, source_target_pairs={{0,2},{2,4},{4,6},{6,8},{8,10},{10,12},{12,14},{14,16},{16,18},{18... | collective-permute-start | bytes 30728 | tf_op jit(solution)/shard_map/ppermute | solution.py:13
  122.6 9.6 %collective-permute-start.15 = (f32[64,4,10,1]{0,2,3,1:T(8,128)S(1)}, f32[64,4,10,1]{0,2,3,1:T(8,128)S(1)}, u32[]{:S(2)}, u32[]{:S(2)}) collective-permute-start(f32[64,4,10,1]{0,2,3,1:T(8,128)S(1)} %copy.28), channel_id=1, source_target_pairs={{2,0},{4,2},{6,4},{8,6},{10,8},{12,10},{14,12},{16,14},{18,16},{20... | collective-permute-start | bytes 30728 | tf_op jit(solution)/shard_map/ppermute | solution.py:13
  133.8 2.4 copy-start.6
  136.6 1.3 copy-start.3
  140.1 8.3 %collective-permute-start.16 = (f32[64,4,1,128]{3,0,2,1:T(8,128)S(1)}, f32[64,4,1,128]{3,0,2,1:T(8,128)S(1)}, u32[]{:S(2)}, u32[]{:S(2)}) collective-permute-start(f32[64,4,1,128]{3,0,2,1:T(8,128)S(1)} %get-tuple-element.16), channel_id=1, source_target_pairs={{0,16},{2,18},{4,20},{6,22},{8,24},{10,26},{12,28},{14,30},{16,32}... | collective-permute-start | bytes 393224 | tf_op jit(solution)/shard_map/ppermute | solution.py:13
  146.5 7.2 %collective-permute-start.17 = (f32[64,4,1,128]{3,0,2,1:T(8,128)S(1)}, f32[64,4,1,128]{3,0,2,1:T(8,128)S(1)}, u32[]{:S(2)}, u32[]{:S(2)}) collective-permute-start(f32[64,4,1,128]{3,0,2,1:T(8,128)S(1)} %get-tuple-element.17), channel_id=1, source_target_pairs={{16,0},{18,2},{20,4},{22,6},{24,8},{26,10},{28,12},{30,14},{32,16}... | collective-permute-start | bytes 393224 | tf_op jit(solution)/shard_map/ppermute | solution.py:13
  157.3 11.7 %collective-permute-start.18 = (f32[64,4,10,1]{0,2,3,1:T(8,128)S(1)}, f32[64,4,10,1]{0,2,3,1:T(8,128)S(1)}, u32[]{:S(2)}, u32[]{:S(2)}) collective-permute-start(f32[64,4,10,1]{0,2,3,1:T(8,128)S(1)} %copy.33), channel_id=1, source_target_pairs={{0,2},{2,4},{4,6},{6,8},{8,10},{10,12},{12,14},{14,16},{16,18},{18... | collective-permute-start | bytes 30728 | tf_op jit(solution)/shard_map/ppermute | solution.py:13
  159.9 9.6 %collective-permute-start.19 = (f32[64,4,10,1]{0,2,3,1:T(8,128)S(1)}, f32[64,4,10,1]{0,2,3,1:T(8,128)S(1)}, u32[]{:S(2)}, u32[]{:S(2)}) collective-permute-start(f32[64,4,10,1]{0,2,3,1:T(8,128)S(1)} %copy.34), channel_id=1, source_target_pairs={{2,0},{4,2},{6,4},{8,6},{10,8},{12,10},{14,12},{16,14},{18,16},{20... | collective-permute-start | bytes 30728 | tf_op jit(solution)/shard_map/ppermute | solution.py:13
  171.1 2.4 copy-start.7
  173.9 1.3 copy-start
  178.0 16.9 %copy-start.8 = (f32[8,128]{1,0:T(8,128)S(1)}, f32[8,128]{1,0:T(8,128)}, u32[]{:S(2)}) copy-start(f32[8,128]{1,0:T(8,128)} %param.8) | copy-start | bytes 12292
Sparse Core Ops, SparseCore 0:
  200.5 140.9 all-reduce.9
where the time goes:
time: 365 us; the launch traced here: 364 us
  waiting for transfers between devices  167 us (46%)
  starting transfers between devices  82.1 us (22%)
  other arithmetic  40.4 us (11%)
  local copies, waits for them, and re-layouts  38.2 us (10%)
  between operations  17.2 us (5%)
  blocking collectives  15.8 us (4%)
    psum x1, waiting for transfers between devices, shards(): gram = lax.psum(gram_local, ('tiles', 'vec'))  140 us
    ppermute x20, starting transfers between devices, shifted(): lax.ppermute(value, axis, [(source, source + steps) for source in range(f...  82 us
    ppermute x20, waiting for transfers between devices, shifted(): lax.ppermute(value, axis, [(source, source + steps) for source in range(f...  27.8 us
    all_to_all x1, blocking collectives, shards(): lax.all_to_all(field, 'vec', split_axis=1, concat_axis=0, tiled=True)  15.8 us
    slice x9, local copies, waits for them, and re-layouts, extend(): left_rim = neighbour(stacked[:, :, :, -margin:], 1)  14.2 us
    another operation x3, other arithmetic, shards(): r_factor = jnp.linalg.cholesky(gram).T  12.4 us
    concatenate x5, other arithmetic, extend(): return jnp.concatenate([left_rim, stacked, right_rim], axis=3)  9.82 us
    ppermute x8, local copies, waits for them, and re-layouts, shifted(): lax.ppermute(value, axis, [(source, source + steps) for source in range(f...  8.08 us
  transfers between devices with their start and end apart: 21, of which 14 were waited for; matrix products, arithmetic and copies ran while one was open for 2% of the time, Pallas kernels for 0%

commit v1 on v0

--- a/solution.py
+++ b/solution.py
@@ -92,7 +92,7 @@
         )
         / total_cells
     )
-    gram = lax.psum(gram_local, ("tiles", "vec"))
+    gram = jnp.sum(lax.all_gather(gram_local, ("tiles", "vec")), axis=0)
     r_factor = jnp.linalg.cholesky(gram).T
     return (field, r_factor)
 

time: 365 us -> 538 us (1.47)
  waiting for transfers between devices: 167 us -> 337 us
    all_gather x0 -> x1, waiting for transfers between devices: none -> 310 us  [shards(): gram = jnp.sum(lax.all_gather(gram_local, ('tiles', 'vec')), axis=0)]
    psum x1 -> x0, waiting for transfers between devices: 140 us -> none  [shards(): gram = lax.psum(gram_local, ('tiles', 'vec'))]
  transfers between devices with their start and end apart: 21 -> 21, of which waited for: 14 -> 14; matrix products, arithmetic and copies ran while one was open for 2% -> 1% of each run, Pallas kernels for 0% -> 0%
where the time goes in v1:
time: 538 us; the launch traced here: 536 us
  waiting for transfers between devices  337 us (63%)
  starting transfers between devices  82.1 us (15%)
  other arithmetic  43.4 us (8%)
  local copies, waits for them, and re-layouts  37.4 us (7%)
  between operations  17.2 us (3%)
  blocking collectives  15.8 us (3%)
    all_gather x1, waiting for transfers between devices, shards(): gram = jnp.sum(lax.all_gather(gram_local, ('tiles', 'vec')), axis=0)  310 us
    ppermute x20, starting transfers between devices, shifted(): lax.ppermute(value, axis, [(source, source + steps) for source in range(f...  82 us
    ppermute x20, waiting for transfers between devices, shifted(): lax.ppermute(value, axis, [(source, source + steps) for source in range(f...  27.8 us
    all_to_all x1, blocking collectives, shards(): lax.all_to_all(field, 'vec', split_axis=1, concat_axis=0, tiled=True)  15.8 us
    slice x9, local copies, waits for them, and re-layouts, extend(): left_rim = neighbour(stacked[:, :, :, -margin:], 1)  14.2 us
    another operation x3, other arithmetic, shards(): r_factor = jnp.linalg.cholesky(gram).T  12.4 us
  transfers between devices with their start and end apart: 21, of which 14 were waited for; matrix products, arithmetic and copies ran while one was open for 1% of the time, Pallas kernels for 0%

profile of v1, /device:TPU:1, one launch (start us, length us, event | category | flops | bytes accessed | tf_op | source)
XLA Modules:
  0.0 536.1 jit_solution(869747838537616942)
XLA Ops:
  7.2 1.5 fusion.34
  14.1 6.3 %collective-permute-start = (f32[4,4,1,128]{3,2,1,0:T(1,128)S(1)}, f32[4,4,1,128]{3,2,1,0:T(1,128)S(1)}, u32[]{:S(2)}, u32[]{:S(2)}) collective-permute-start(f32[4,4,1,128]{3,2,1,0:T(1,128)S(1)} %get-tuple-element.29), channel_id=1, source_target_pairs={{0,16},{2,18},{4,20},{6,22},{8,24},{10,26},{12,28},{14,30},{16,32}... | collective-permute-start | bytes 24584 | tf_op jit(solution)/shard_map/ppermute | solution.py:13
  21.7 1.8 copy_multiply_fusion
  23.6 2.7 collective-permute-done.1
  26.4 5.1 collective-permute-start.2
  31.6 1.9 collective-permute-start.3
  33.5 3.2 collective-permute-start.4
  38.6 5.3 collective-permute-done.5
  44.0 1.5 fusion.28
  45.6 2.0 copy.13
  48.3 8.0 %collective-permute-start.7 = (f32[64,4,10,1]{0,2,3,1:T(8,128)S(1)}, f32[64,4,10,1]{0,2,3,1:T(8,128)S(1)}, u32[]{:S(2)}, u32[]{:S(2)}) collective-permute-start(f32[64,4,10,1]{0,2,3,1:T(8,128)S(1)} %copy.14), channel_id=1, source_target_pairs={{2,0},{4,2},{6,4},{8,6},{10,8},{12,10},{14,12},{16,14},{18,16},{20... | collective-permute-start | bytes 30728 | tf_op jit(solution)/shard_map/ppermute | solution.py:13
  56.2 1.9 collective-permute-start.6
  59.8 1.6 copy.16
  61.4 2.4 pad_maximum_fusion
  66.7 1.3 fusion.23
  68.0 6.0 %collective-permute-start.8 = (f32[64,4,1,128]{3,0,2,1:T(8,128)S(1)}, f32[64,4,1,128]{3,0,2,1:T(8,128)S(1)}, u32[]{:S(2)}, u32[]{:S(2)}) collective-permute-start(f32[64,4,1,128]{3,0,2,1:T(8,128)S(1)} %get-tuple-element.20), channel_id=1, source_target_pairs={{0,16},{2,18},{4,20},{6,22},{8,24},{10,26},{12,28},{14,30},{16,32}... | collective-permute-start | bytes 393224 | tf_op jit(solution)/shard_map/ppermute | solution.py:13
  76.0 5.3 collective-permute-done.9
  81.4 1.5 fusion.27
  82.9 2.0 copy.19
  84.9 5.5 %collective-permute-start.10 = (f32[64,4,10,1]{0,2,3,1:T(8,128)S(1)}, f32[64,4,10,1]{0,2,3,1:T(8,128)S(1)}, u32[]{:S(2)}, u32[]{:S(2)}) collective-permute-start(f32[64,4,10,1]{0,2,3,1:T(8,128)S(1)} %copy.19), channel_id=1, source_target_pairs={{0,2},{2,4},{4,6},{6,8},{8,10},{10,12},{12,14},{14,16},{16,18},{18... | collective-permute-start | bytes 30728 | tf_op jit(solution)/shard_map/ppermute | solution.py:13
  91.1 5.1 collective-permute-start.11
  96.9 1.6 copy.22
  98.4 2.4 pad_maximum_fusion.1
  103.3 1.3 fusion.20
  104.7 4.5 collective-permute-start.12
  111.1 5.3 collective-permute-done.13
  116.5 1.5 fusion.26
  118.0 2.0 copy.25
  120.0 1.9 collective-permute-start.14
  122.6 8.8 %collective-permute-start.15 = (f32[64,4,10,1]{0,2,3,1:T(8,128)S(1)}, f32[64,4,10,1]{0,2,3,1:T(8,128)S(1)}, u32[]{:S(2)}, u32[]{:S(2)}) collective-permute-start(f32[64,4,10,1]{0,2,3,1:T(8,128)S(1)} %copy.26), channel_id=1, source_target_pairs={{2,0},{4,2},{6,4},{8,6},{10,8},{12,10},{14,12},{16,14},{18,16},{20... | collective-permute-start | bytes 30728 | tf_op jit(solution)/shard_map/ppermute | solution.py:13
  132.3 1.6 copy.28
  133.8 2.4 pad_maximum_fusion.2
  138.8 1.3 fusion.17
  140.1 6.4 %collective-permute-start.16 = (f32[64,4,1,128]{3,0,2,1:T(8,128)S(1)}, f32[64,4,1,128]{3,0,2,1:T(8,128)S(1)}, u32[]{:S(2)}, u32[]{:S(2)}) collective-permute-start(f32[64,4,1,128]{3,0,2,1:T(8,128)S(1)} %get-tuple-element.16), channel_id=1, source_target_pairs={{0,16},{2,18},{4,20},{6,22},{8,24},{10,26},{12,28},{14,30},{16,32}... | collective-permute-start | bytes 393224 | tf_op jit(solution)/shard_map/ppermute | solution.py:13
  148.4 5.3 collective-permute-done.17
  153.8 1.5 fusion.25
  155.3 2.0 copy.31
  157.3 1.9 collective-permute-start.18
  159.9 9.0 %collective-permute-start.19 = (f32[64,4,10,1]{0,2,3,1:T(8,128)S(1)}, f32[64,4,10,1]{0,2,3,1:T(8,128)S(1)}, u32[]{:S(2)}, u32[]{:S(2)}) collective-permute-start(f32[64,4,10,1]{0,2,3,1:T(8,128)S(1)} %copy.32), channel_id=1, source_target_pairs={{2,0},{4,2},{6,4},{8,6},{10,8},{12,10},{14,12},{16,14},{18,16},{20... | collective-permute-start | bytes 30728 | tf_op jit(solution)/shard_map/ppermute | solution.py:13
  169.6 1.6 copy.34
  171.1 2.4 pad_maximum_fusion.3
  178.0 15.8 %all_to_all.15 = f32[64,4,8,128]{3,2,0,1:T(8,128)S(1)} all-to-all(f32[64,4,8,128]{3,2,0,1:T(8,128)S(1)} %copy.37), channel_id=1, replica_groups=mesh['tiles'=64,'vec'=2] {'vec'}, dimensions={1} | all-to-all | bytes 2097152 | tf_op jit(solution)/shard_map/all_to_all | solution.py:80
  194.9 1.4 reshape.96
  197.5 2.9 convolution_multiply_fusion
  200.3 1.6 copy.40
  201.9 309.6 %all-gather.3.cloned.1.call-done = f32[16384,128]{1,0:T(8,128)} async-done(((f32[128,128]{1,0:T(8,128)}), f32[16384,128]{1,0:T(8,128)}) %all-gather.3.cloned.1.call-update) | async-done | bytes 8388624 | tf_op jit(solution)/shard_map/all_gather | solution.py:95
  511.5 3.8 reduce_sum.9
  515.5 11.7 %cholesky.18 = f32[128,128]{1,0:T(8,128)S(1)} custom-call(f32[128,128]{1,0:T(8,128)S(1)} %fusion.24), custom_call_target="Cholesky" | custom-call | tf_op jit(solution)/shard_map/jit(cholesky)/cholesky | solution.py:96
  (97 shorter events, 35.4 us)
Async XLA Ops:
  7.2 504.4 %all-gather.3.cloned.1.call-start = ((), (), s32[]{:S(2)}) async-start(), calls=%async_computation.1 | async-start | bytes 8454144 | tf_op jit(solution)/shard_map/all_gather | solution.py:95
  14.1 9.5 %collective-permute-start = (f32[4,4,1,128]{3,2,1,0:T(1,128)S(1)}, f32[4,4,1,128]{3,2,1,0:T(1,128)S(1)}, u32[]{:S(2)}, u32[]{:S(2)}) collective-permute-start(f32[4,4,1,128]{3,2,1,0:T(1,128)S(1)} %get-tuple-element.29), channel_id=1, source_target_pairs={{0,16},{2,18},{4,20},{6,22},{8,24},{10,26},{12,28},{14,30},{16,32}... | collective-permute-start | bytes 24584 | tf_op jit(solution)/shard_map/ppermute | solution.py:13
  20.4 5.9 %collective-permute-start.1 = (f32[4,4,1,128]{3,2,1,0:T(1,128)S(1)}, f32[4,4,1,128]{3,2,1,0:T(1,128)S(1)}, u32[]{:S(2)}, u32[]{:S(2)}) collective-permute-start(f32[4,4,1,128]{3,2,1,0:T(1,128)S(1)} %get-tuple-element.30), channel_id=1, source_target_pairs={{16,0},{18,2},{20,4},{22,6},{24,8},{26,10},{28,12},{30,14},{32,16}... | collective-permute-start | bytes 24584 | tf_op jit(solution)/shard_map/ppermute | solution.py:13
  26.4 11.6 %collective-permute-start.2 = (f32[4,4,10,1]{3,2,1,0:T(8,128)S(1)}, f32[4,4,10,1]{3,2,1,0:T(8,128)S(1)}, u32[]{:S(2)}, u32[]{:S(2)}) collective-permute-start(f32[4,4,10,1]{3,2,1,0:T(8,128)S(1)} %get-tuple-element.27), channel_id=1, source_target_pairs={{0,2},{2,4},{4,6},{6,8},{8,10},{10,12},{12,14},{14,16},{16,18},{18... | collective-permute-start | bytes 1928 | tf_op jit(solution)/shard_map/ppermute | solution.py:13
  31.6 6.5 %collective-permute-start.3 = (f32[4,4,10,1]{3,2,1,0:T(8,128)S(1)}, f32[4,4,10,1]{3,2,1,0:T(8,128)S(1)}, u32[]{:S(2)}, u32[]{:S(2)}) collective-permute-start(f32[4,4,10,1]{3,2,1,0:T(8,128)S(1)} %get-tuple-element.28), channel_id=1, source_target_pairs={{2,0},{4,2},{6,4},{8,6},{10,8},{12,10},{14,12},{16,14},{18,16},{20... | collective-permute-start | bytes 1928 | tf_op jit(solution)/shard_map/ppermute | solution.py:13
  33.5 5.1 collective-permute-start.4
  36.7 7.2 %collective-permute-start.5 = (f32[64,4,1,128]{3,0,2,1:T(8,128)S(1)}, f32[64,4,1,128]{3,0,2,1:T(8,128)S(1)}, u32[]{:S(2)}, u32[]{:S(2)}) collective-permute-start(f32[64,4,1,128]{3,0,2,1:T(8,128)S(1)} %get-tuple-element.23), channel_id=1, source_target_pairs={{16,0},{18,2},{20,4},{22,6},{24,8},{26,10},{28,12},{30,14},{32,16}... | collective-permute-start | bytes 393224 | tf_op jit(solution)/shard_map/ppermute | solution.py:13
  48.3 11.5 %collective-permute-start.7 = (f32[64,4,10,1]{0,2,3,1:T(8,128)S(1)}, f32[64,4,10,1]{0,2,3,1:T(8,128)S(1)}, u32[]{:S(2)}, u32[]{:S(2)}) collective-permute-start(f32[64,4,10,1]{0,2,3,1:T(8,128)S(1)} %copy.14), channel_id=1, source_target_pairs={{2,0},{4,2},{6,4},{8,6},{10,8},{12,10},{14,12},{16,14},{18,16},{20... | collective-permute-start | bytes 30728 | tf_op jit(solution)/shard_map/ppermute | solution.py:13
  56.2 3.1 collective-permute-start.6
  58.2 42.7 %copy-start.5 = (f32[3,10,130]{2,1,0:T(8,128)}, f32[3,10,130]{2,1,0:T(8,128)S(1)}, u32[]{:S(2)}) copy-start(f32[3,10,130]{2,1,0:T(8,128)S(1)} %slice_bitcast_fusion.3) | copy-start | bytes 46804
  64.1 1.3 copy-start.1
  65.5 1.2 copy-start.4
  68.0 8.0 %collective-permute-start.8 = (f32[64,4,1,128]{3,0,2,1:T(8,128)S(1)}, f32[64,4,1,128]{3,0,2,1:T(8,128)S(1)}, u32[]{:S(2)}, u32[]{:S(2)}) collective-permute-start(f32[64,4,1,128]{3,0,2,1:T(8,128)S(1)} %get-tuple-element.20), channel_id=1, source_target_pairs={{0,16},{2,18},{4,20},{6,22},{8,24},{10,26},{12,28},{14,30},{16,32}... | collective-permute-start | bytes 393224 | tf_op jit(solution)/shard_map/ppermute | solution.py:13
  74.1 7.2 %collective-permute-start.9 = (f32[64,4,1,128]{3,0,2,1:T(8,128)S(1)}, f32[64,4,1,128]{3,0,2,1:T(8,128)S(1)}, u32[]{:S(2)}, u32[]{:S(2)}) collective-permute-start(f32[64,4,1,128]{3,0,2,1:T(8,128)S(1)} %get-tuple-element.21), channel_id=1, source_target_pairs={{16,0},{18,2},{20,4},{22,6},{24,8},{26,10},{28,12},{30,14},{32,16}... | collective-permute-start | bytes 393224 | tf_op jit(solution)/shard_map/ppermute | solution.py:13
  84.9 11.3 %collective-permute-start.10 = (f32[64,4,10,1]{0,2,3,1:T(8,128)S(1)}, f32[64,4,10,1]{0,2,3,1:T(8,128)S(1)}, u32[]{:S(2)}, u32[]{:S(2)}) collective-permute-start(f32[64,4,10,1]{0,2,3,1:T(8,128)S(1)} %copy.19), channel_id=1, source_target_pairs={{0,2},{2,4},{4,6},{6,8},{8,10},{10,12},{12,14},{14,16},{16,18},{18... | collective-permute-start | bytes 30728 | tf_op jit(solution)/shard_map/ppermute | solution.py:13
  91.1 5.8 %collective-permute-start.11 = (f32[64,4,10,1]{0,2,3,1:T(8,128)S(1)}, f32[64,4,10,1]{0,2,3,1:T(8,128)S(1)}, u32[]{:S(2)}, u32[]{:S(2)}) collective-permute-start(f32[64,4,10,1]{0,2,3,1:T(8,128)S(1)} %copy.20), channel_id=1, source_target_pairs={{2,0},{4,2},{6,4},{8,6},{10,8},{12,10},{14,12},{16,14},{18,16},{20... | collective-permute-start | bytes 30728 | tf_op jit(solution)/shard_map/ppermute | solution.py:13
  101.2 1.3 copy-start.2
  104.7 6.4 %collective-permute-start.12 = (f32[64,4,1,128]{3,0,2,1:T(8,128)S(1)}, f32[64,4,1,128]{3,0,2,1:T(8,128)S(1)}, u32[]{:S(2)}, u32[]{:S(2)}) collective-permute-start(f32[64,4,1,128]{3,0,2,1:T(8,128)S(1)} %get-tuple-element.18), channel_id=1, source_target_pairs={{0,16},{2,18},{4,20},{6,22},{8,24},{10,26},{12,28},{14,30},{16,32}... | collective-permute-start | bytes 393224 | tf_op jit(solution)/shard_map/ppermute | solution.py:13
  109.2 7.2 %collective-permute-start.13 = (f32[64,4,1,128]{3,0,2,1:T(8,128)S(1)}, f32[64,4,1,128]{3,0,2,1:T(8,128)S(1)}, u32[]{:S(2)}, u32[]{:S(2)}) collective-permute-start(f32[64,4,1,128]{3,0,2,1:T(8,128)S(1)} %get-tuple-element.19), channel_id=1, source_target_pairs={{16,0},{18,2},{20,4},{22,6},{24,8},{26,10},{28,12},{30,14},{32,16}... | collective-permute-start | bytes 393224 | tf_op jit(solution)/shard_map/ppermute | solution.py:13
  120.0 11.4 %collective-permute-start.14 = (f32[64,4,10,1]{0,2,3,1:T(8,128)S(1)}, f32[64,4,10,1]{0,2,3,1:T(8,128)S(1)}, u32[]{:S(2)}, u32[]{:S(2)}) collective-permute-start(f32[64,4,10,1]{0,2,3,1:T(8,128)S(1)} %copy.25), channel_id=1, source_target_pairs={{0,2},{2,4},{4,6},{6,8},{8,10},{10,12},{12,14},{14,16},{16,18},{18... | collective-permute-start | bytes 30728 | tf_op jit(solution)/shard_map/ppermute | solution.py:13
  122.6 9.6 %collective-permute-start.15 = (f32[64,4,10,1]{0,2,3,1:T(8,128)S(1)}, f32[64,4,10,1]{0,2,3,1:T(8,128)S(1)}, u32[]{:S(2)}, u32[]{:S(2)}) collective-permute-start(f32[64,4,10,1]{0,2,3,1:T(8,128)S(1)} %copy.26), channel_id=1, source_target_pairs={{2,0},{4,2},{6,4},{8,6},{10,8},{12,10},{14,12},{16,14},{18,16},{20... | collective-permute-start | bytes 30728 | tf_op jit(solution)/shard_map/ppermute | solution.py:13
  133.8 2.4 copy-start.6
  136.6 1.3 copy-start.3
  140.1 8.3 %collective-permute-start.16 = (f32[64,4,1,128]{3,0,2,1:T(8,128)S(1)}, f32[64,4,1,128]{3,0,2,1:T(8,128)S(1)}, u32[]{:S(2)}, u32[]{:S(2)}) collective-permute-start(f32[64,4,1,128]{3,0,2,1:T(8,128)S(1)} %get-tuple-element.16), channel_id=1, source_target_pairs={{0,16},{2,18},{4,20},{6,22},{8,24},{10,26},{12,28},{14,30},{16,32}... | collective-permute-start | bytes 393224 | tf_op jit(solution)/shard_map/ppermute | solution.py:13
  146.5 7.2 %collective-permute-start.17 = (f32[64,4,1,128]{3,0,2,1:T(8,128)S(1)}, f32[64,4,1,128]{3,0,2,1:T(8,128)S(1)}, u32[]{:S(2)}, u32[]{:S(2)}) collective-permute-start(f32[64,4,1,128]{3,0,2,1:T(8,128)S(1)} %get-tuple-element.17), channel_id=1, source_target_pairs={{16,0},{18,2},{20,4},{22,6},{24,8},{26,10},{28,12},{30,14},{32,16}... | collective-permute-start | bytes 393224 | tf_op jit(solution)/shard_map/ppermute | solution.py:13
  157.3 11.7 %collective-permute-start.18 = (f32[64,4,10,1]{0,2,3,1:T(8,128)S(1)}, f32[64,4,10,1]{0,2,3,1:T(8,128)S(1)}, u32[]{:S(2)}, u32[]{:S(2)}) collective-permute-start(f32[64,4,10,1]{0,2,3,1:T(8,128)S(1)} %copy.31), channel_id=1, source_target_pairs={{0,2},{2,4},{4,6},{6,8},{8,10},{10,12},{12,14},{14,16},{16,18},{18... | collective-permute-start | bytes 30728 | tf_op jit(solution)/shard_map/ppermute | solution.py:13
  159.9 9.6 %collective-permute-start.19 = (f32[64,4,10,1]{0,2,3,1:T(8,128)S(1)}, f32[64,4,10,1]{0,2,3,1:T(8,128)S(1)}, u32[]{:S(2)}, u32[]{:S(2)}) collective-permute-start(f32[64,4,10,1]{0,2,3,1:T(8,128)S(1)} %copy.32), channel_id=1, source_target_pairs={{2,0},{4,2},{6,4},{8,6},{10,8},{12,10},{14,12},{16,14},{18,16},{20... | collective-permute-start | bytes 30728 | tf_op jit(solution)/shard_map/ppermute | solution.py:13
  171.1 2.4 copy-start.7
  173.9 1.3 copy-start
  178.0 16.9 %copy-start.8 = (f32[8,128]{1,0:T(8,128)S(1)}, f32[8,128]{1,0:T(8,128)}, u32[]{:S(2)}) copy-start(f32[8,128]{1,0:T(8,128)} %param.8) | copy-start | bytes 12292
Sparse Core Ops, SparseCore 0:
  200.5 311.0 all-gather.2
